TPU v7x, 256 devices: a whole 4x4x8 slice. The times are simulated.
256 devices in a mesh: row: 16 (over z, core), col: 16 (over y, x).
Axes of the slice: x: 4, y: 4, z: 8, core: 2. Of those that a mesh axis runs over, the one named last changes fastest.
Arguments:
- clean_in: bfloat16 [512, 8192], P('row', 'col'), may hold values from -6 to 6
- corrupt_in: bfloat16 [512, 8192], P('row', 'col'), may hold values from -6 to 6
- patch_mask: int32 [512], replicated, may hold values 0 or 1
- gate_weight: bfloat16 [8192, 28672], P('col', 'row'), may hold values from -0.0625 to 0.0625
- up_weight: bfloat16 [8192, 28672], P('col', 'row'), may hold values from -0.0625 to 0.0625
- down_weight: bfloat16 [28672, 8192], P('row', 'col'), may hold values from -0.03125 to 0.03125
Outputs:
- clean_out: float32 [512, 8192], P('row', 'col')
- patched_out: float32 [512, 8192], P('row', 'col')
All inputs are finite; a program needn't handle non-finite values.
Results may differ from a plain program's by a relative error of at most 0.0029.
Values may be sent and summed in bfloat16 or wider, within the bound.
A program may use at most 128 MiB of HBM per device.

v0:
```python
import jax
import jax.numpy as jnp
from jax import lax
from jax.sharding import PartitionSpec as P


def on_device(clean_in, corrupt_in, patch_mask, gate_weight, up_weight, down_weight):
    stacked = jnp.stack((clean_in, corrupt_in), axis=1)
    piece = lax.all_gather(stacked, "row", axis=0, tiled=True)
    gate_part = jnp.einsum("tkd,df->tkf", piece, gate_weight, preferred_element_type=jnp.float32)
    up_part = jnp.einsum("tkd,df->tkf", piece, up_weight, preferred_element_type=jnp.float32)
    partial_sums = jnp.stack((gate_part, up_part), axis=2)
    summed = lax.psum_scatter(partial_sums, "col", scatter_dimension=0, tiled=True)
    row_count = summed.shape[0]
    row_mask = lax.dynamic_slice_in_dim(patch_mask, lax.axis_index("col") * row_count, row_count, 0)
    hidden = (jax.nn.silu(summed[:, :, 0]) * summed[:, :, 1]).astype(jnp.bfloat16)
    patched = jnp.where(row_mask[:, None] == 1, hidden[:, 0], hidden[:, 1])
    paired = jnp.stack((hidden[:, 0], patched), axis=1)
    gathered = lax.all_gather(paired, "col", axis=0, tiled=True)
    result = lax.psum_scatter(
        jnp.einsum("tkf,fd->tkd", gathered, down_weight, preferred_element_type=jnp.float32),
        "row",
        scatter_dimension=0,
        tiled=True,
    )
    return (result[:, 0], result[:, 1])


def solution(mesh):
    placed = (
        P("row", "col"),
        P("row", "col"),
        P(),
        P("col", "row"),
        P("col", "row"),
        P("row", "col"),
    )
    return jax.shard_map(
        on_device,
        mesh=mesh,
        in_specs=placed,
        out_specs=(P("row", "col"), P("row", "col")),
        check_vma=False,
    )
```

profile of v0, /device:TPU:2, one launch (start us, length us, event | category | flops | bytes accessed | tf_op | source)
XLA Modules:
  0.0 311.0 jit_solution(6040133685950640488)
XLA Ops:
  7.2 0.0 copy-start
  7.2 0.0 all-gather.3.cloned.1.call-start
  7.2 1.5 pad_maximum_fusion.2
  8.8 0.0 all-gather.3.cloned.1.call-update
  8.8 0.0 reduce-scatter.3.cloned.1.call-start
  8.8 43.1 %all-gather.3.cloned.1.call-done = bf16[512,2,512]{2,0,1:T(8,128)(2,1)} async-done(((bf16[32,2,512]{2,0,1:T(8,128)(2,1)}), bf16[512,2,512]{2,0,1:T(8,128)(2,1)}) %all-gather.3.cloned.1.call-update) | async-done | bytes 1048592 | tf_op jit(solution)/shard_map/all_gather | solution.py:9
  52.0 0.0 copy-done
  52.0 0.0 copy-start.1
  52.0 0.0 copy-start.2
  52.0 6.4 %convolution_bitcast_fusion = f32[512,2,1,1792]{3,0,1,2:T(8,128)} fusion(bf16[512,2,512]{2,0,1:T(8,128)(2,1)} %all-gather.3.cloned.1.call-done, bf16[512,1792]{1,0:T(8,128)(2,1)S(1)} %copy-done), kind=kOutput, calls=%fused_computation.1 | convolution fusion | flops 1879048192 | bytes 10223616 | tf_op jit(solution)/shard_map/tkd,df->tkf/dot_general | solution.py:11
  58.3 0.0 copy-done.1
  58.3 0.0 copy-done.2
  58.3 5.0 %convolution_bitcast_fusion.1 = f32[512,2,1,1792]{3,0,1,2:T(8,128)} fusion(bf16[512,2,512]{2,0,1:T(8,128)(2,1)S(1)} %copy-done.2, bf16[512,1792]{1,0:T(8,128)(2,1)S(1)} %copy-done.1), kind=kOutput, calls=%fused_computation.2 | convolution fusion | flops 1879048192 | bytes 10223616 | tf_op jit(solution)/shard_map/tkd,df->tkf/dot_general | solution.py:10
  63.4 11.9 %pad_maximum_fusion = f32[512,2,2,1792]{3,0,1,2:T(8,128)} fusion(f32[512,2,1,1792]{3,0,1,2:T(8,128)} %convolution_bitcast_fusion, f32[512,2,1,1792]{3,0,1,2:T(8,128)} %convolution_bitcast_fusion.1), kind=kLoop, calls=%fused_computation | loop fusion | flops 3670016 | bytes 29360128 | tf_op jit(solution)/shard_map/stack | solution.py:12
  75.3 0.0 reduce-scatter.3.cloned.1.call-update
  75.3 0.0 all-gather.5.cloned.1.call-start
  75.3 0.8 dynamic-slice_compare_fusion
  76.1 104.8 %reduce-scatter.3.cloned.1.call-done = f32[32,2,2,1792]{3,0,1,2:T(8,128)} async-done(((f32[512,2,2,1792]{3,0,1,2:T(8,128)}), f32[32,2,2,1792]{3,0,1,2:T(8,128)}) %reduce-scatter.3.cloned.1.call-update) | async-done | bytes 917520 | tf_op jit(solution)/shard_map/reduce_scatter | solution.py:13
  180.9 1.3 fusion.5
  182.2 0.1 fusion.6
  182.3 0.7 pad_maximum_fusion.1
  183.0 0.0 all-gather.5.cloned.1.call-update
  183.0 0.0 reduce-scatter.5.cloned.1.call-start
  183.1 54.0 %all-gather.5.cloned.1.call-done = bf16[512,2,1792]{2,0,1:T(8,128)(2,1)} async-done(((bf16[32,2,1792]{2,0,1:T(8,128)(2,1)}), bf16[512,2,1792]{2,0,1:T(8,128)(2,1)}) %all-gather.5.cloned.1.call-update) | async-done | bytes 3670032 | tf_op jit(solution)/shard_map/all_gather | solution.py:19
  237.0 6.0 %fusion = f32[512,2,512]{2,0,1:T(8,128)} fusion(bf16[512,2,1792]{2,0,1:T(8,128)(2,1)} %all-gather.5.cloned.1.call-done, bf16[1792,512]{1,0:T(8,128)(2,1)} %param.11), kind=kOutput, calls=%fused_computation.3 | convolution fusion | flops 1879048192 | bytes 7602176 | tf_op jit(solution)/shard_map/tkf,fd->tkd/dot_general | solution.py:21
  243.0 0.0 reduce-scatter.5.cloned.1.call-update
  243.1 59.8 %reduce-scatter.5.cloned.1.call-done = f32[32,2,512]{2,0,1:T(8,128)} async-done(((f32[512,2,512]{2,0,1:T(8,128)}), f32[32,2,512]{2,0,1:T(8,128)}) %reduce-scatter.5.cloned.1.call-update) | async-done | bytes 131088 | tf_op jit(solution)/shard_map/reduce_scatter | solution.py:20
  302.9 1.5 slice_bitcast_fusion.2
Async XLA Ops:
  7.2 44.8 %copy-start = (bf16[512,1792]{1,0:T(8,128)(2,1)S(1)}, bf16[512,1792]{1,0:T(8,128)(2,1)}, u32[]{:S(2)}) copy-start(bf16[512,1792]{1,0:T(8,128)(2,1)} %param.10) | copy-start | bytes 5505028
  7.2 44.8 %all-gather.3.cloned.1.call-start = ((), (), s32[]{:S(2)}) async-start(), calls=%async_computation.2 | async-start | bytes 1114112 | tf_op jit(solution)/shard_map/all_gather | solution.py:9
  8.8 172.1 %reduce-scatter.3.cloned.1.call-start = ((), (), s32[]{:S(2)}) async-start(), calls=%async_computation.3 | async-start | bytes 15597568 | tf_op jit(solution)/shard_map/reduce_scatter | solution.py:13
  52.0 6.4 %copy-start.1 = (bf16[512,1792]{1,0:T(8,128)(2,1)S(1)}, bf16[512,1792]{1,0:T(8,128)(2,1)}, u32[]{:S(2)}) copy-start(bf16[512,1792]{1,0:T(8,128)(2,1)} %param.9) | copy-start | bytes 5505028
  52.0 6.4 %copy-start.2 = (bf16[512,2,512]{2,0,1:T(8,128)(2,1)S(1)}, bf16[512,2,512]{2,0,1:T(8,128)(2,1)}, u32[]{:S(2)}) copy-start(bf16[512,2,512]{2,0,1:T(8,128)(2,1)} %all-gather.3.cloned.1.call-done) | copy-start | bytes 3145732
  75.3 161.8 %all-gather.5.cloned.1.call-start = ((), (), s32[]{:S(2)}) async-start(), calls=%async_computation.4 | async-start | bytes 3899392 | tf_op jit(solution)/shard_map/all_gather | solution.py:19
  183.0 119.9 %reduce-scatter.5.cloned.1.call-start = ((), (), s32[]{:S(2)}) async-start(), calls=%async_computation.5 | async-start | bytes 2228224 | tf_op jit(solution)/shard_map/reduce_scatter | solution.py:20
Sparse Core Ops, SparseCore 0:
  10.4 41.5 all-gather.2
  75.4 105.4 reduce-scatter.2
  183.3 53.6 all-gather.4
  243.2 59.6 reduce-scatter.4
where the time goes:
time: 311 us
  waiting for transfers between devices  262 us (84%)
  matrix products  17.4 us (6%)
  other arithmetic  16.3 us (5%)
  between operations  13.8 us (4%)
    reduce_scatter x1, waiting for transfers between devices, on_device(): lax.psum_scatter(partial_sums, 'col', scatter_dimension=0, tiled=True)  105 us
    reduce_scatter x1, waiting for transfers between devices, on_device(): lax.psum_scatter(jnp.einsum('tkf,fd->tkd', gathered, down_weight, preferr...  59.8 us
    all_gather x1, waiting for transfers between devices, on_device(): gathered = lax.all_gather(paired, 'col', axis=0, tiled=True)  54 us
    all_gather x1, waiting for transfers between devices, on_device(): piece = lax.all_gather(stacked, 'row', axis=0, tiled=True)  43.1 us
    another operation x1, other arithmetic, on_device(): partial_sums = jnp.stack((gate_part, up_part), axis=2)  11.9 us
    dot_general x1, matrix products, on_device(): jnp.einsum('tkd,df->tkf', piece, up_weight, preferred_element_type=jnp.fl...  6.36 us
  transfers between devices with their start and end apart: 4, of which 4 were waited for; matrix products, arithmetic and copies ran while one was open for 0% of the time, Pallas kernels for 0%

commit v1 on v0

--- a/solution.py
+++ b/solution.py
@@ -6,7 +6,20 @@
 
 def on_device(clean_in, corrupt_in, patch_mask, gate_weight, up_weight, down_weight):
     stacked = jnp.stack((clean_in, corrupt_in), axis=1)
-    piece = lax.all_gather(stacked, "row", axis=0, tiled=True)
+    ways, here, step = (lax.axis_size("row"), lax.axis_index("row"), stacked.shape[0])
+    dims = [n * ways if d == 0 else n for d, n in enumerate(stacked.shape)]
+    piece = lax.dynamic_update_slice_in_dim(
+        jnp.zeros(dims, stacked.dtype), stacked, here * step, axis=0
+    )
+    going_up = going_down = stacked
+    for far in range(1, ways // 2 + 1):
+        going_up = lax.ppermute(going_up, "row", [(d, (d + 1) % ways) for d in range(ways)])
+        piece = lax.dynamic_update_slice_in_dim(piece, going_up, (here - far) % ways * step, axis=0)
+        if 2 * far < ways:
+            going_down = lax.ppermute(going_down, "row", [(d, (d - 1) % ways) for d in range(ways)])
+            piece = lax.dynamic_update_slice_in_dim(
+                piece, going_down, (here + far) % ways * step, axis=0
+            )
     gate_part = jnp.einsum("tkd,df->tkf", piece, gate_weight, preferred_element_type=jnp.float32)
     up_part = jnp.einsum("tkd,df->tkf", piece, up_weight, preferred_element_type=jnp.float32)
     partial_sums = jnp.stack((gate_part, up_part), axis=2)

time: 311 us -> 310 us (level)
  starting transfers between devices: 0.16 us -> 23.3 us
  waiting for transfers between devices: 262 us -> 239 us
    all_gather x1 -> x0, waiting for transfers between devices: 43.1 us -> none  [on_device(): piece = lax.all_gather(stacked, 'row', axis=0, tiled=True)]
    ppermute x0 -> x15, starting transfers between devices: none -> 23.2 us  [the longest x7 23.1 us: on_device(): lax.ppermute(going_down, 'row', [(d, (d - 1) % ways) for d in range(ways)])]
    ppermute x0 -> x15, waiting for transfers between devices: none -> 18.2 us  [the longest x8 18.1 us: on_device(): lax.ppermute(going_up, 'row', [(d, (d + 1) % ways) for d in range(ways)])]
  transfers between devices with their start and end apart: 4 -> 18, of which waited for: 4 -> 11; matrix products, arithmetic and copies ran while one was open for 0% -> 0% of each run, Pallas kernels for 0% -> 0%
where the time goes in v1:
time: 310 us; the launch traced here: 309 us
  waiting for transfers between devices  239 us (77%)
  starting transfers between devices  23.3 us (8%)
  matrix products  16 us (5%)
  other arithmetic  15.7 us (5%)
  between operations  13.9 us (4%)
    reduce_scatter x1, waiting for transfers between devices, on_device(): lax.psum_scatter(partial_sums, 'col', scatter_dimension=0, tiled=True)  107 us
    reduce_scatter x1, waiting for transfers between devices, on_device(): lax.psum_scatter(jnp.einsum('tkf,fd->tkd', gathered, down_weight, preferr...  59.8 us
    all_gather x1, waiting for transfers between devices, on_device(): gathered = lax.all_gather(paired, 'col', axis=0, tiled=True)  54 us
    ppermute x7, starting transfers between devices, on_device(): lax.ppermute(going_down, 'row', [(d, (d - 1) % ways) for d in range(ways)])  23.1 us
    ppermute x8, waiting for transfers between devices, on_device(): lax.ppermute(going_up, 'row', [(d, (d + 1) % ways) for d in range(ways)])  18.1 us
    another operation x1, other arithmetic, on_device(): partial_sums = jnp.stack((gate_part, up_part), axis=2)  11.9 us
  transfers between devices with their start and end apart: 18, of which 11 were waited for; matrix products, arithmetic and copies ran while one was open for 0% of the time, Pallas kernels for 0%

profile of v1, /device:TPU:2, one launch (start us, length us, event | category | flops | bytes accessed | tf_op | source)
XLA Modules:
  0.0 309.3 jit_solution(6225265835234675924)
XLA Ops:
  7.2 0.0 reduce-scatter.3.cloned.1.call-start
  7.2 0.1 broadcast_in_dim.12
  7.3 0.9 pad_maximum_fusion.2
  8.2 5.3 %collective-permute-start.1 = (bf16[32,2,512]{2,0,1:T(8,128)(2,1)S(1)}, bf16[32,2,512]{2,0,1:T(8,128)(2,1)S(1)}, u32[]{:S(2)}, u32[]{:S(2)}) collective-permute-start(bf16[32,2,512]{2,0,1:T(8,128)(2,1)S(1)} %get-tuple-element.6), channel_id=1, source_target_pairs={{0,240},{16,0},{32,16},{48,32},{64,48},{80,64},{96,80},{112,96},{1... | collective-permute-start | bytes 196616 | tf_op jit(solution)/shard_map/ppermute | solution.py:19
  13.5 1.9 collective-permute-done
  15.5 3.0 collective-permute-start.3
  18.5 1.9 collective-permute-done.2
  20.4 3.0 collective-permute-start.5
  23.4 1.9 collective-permute-done.4
  25.3 3.0 collective-permute-start.7
  28.3 1.9 collective-permute-done.6
  30.2 3.0 collective-permute-start.9
  33.2 1.9 collective-permute-done.8
  35.1 3.0 collective-permute-start.11
  38.1 1.9 collective-permute-done.10
  40.0 3.0 collective-permute-start.13
  43.0 1.9 collective-permute-done.12
  44.9 4.9 %collective-permute-done.14 = bf16[32,2,512]{2,0,1:T(8,128)(2,1)S(1)} collective-permute-done((bf16[32,2,512]{2,0,1:T(8,128)(2,1)S(1)}, bf16[32,2,512]{2,0,1:T(8,128)(2,1)S(1)}, u32[]{:S(2)}, u32[]{:S(2)}) %collective-permute-start.14) | collective-permute-done | bytes 65568 | tf_op jit(solution)/shard_map/ppermute | solution.py:16
  49.8 5.0 %convolution_bitcast_fusion = f32[512,2,1,1792]{3,0,1,2:T(8,128)} fusion(bf16[512,2,512]{2,0,1:T(8,128)(2,1)S(1)} %constant_dynamic-update-slice_fusion, bf16[512,1792]{1,0:T(8,128)(2,1)S(1)} %copy-done), kind=kOutput, calls=%fused_computation.1 | convolution fusion | flops 1879048192 | bytes 10223616 | tf_op jit(solution)/shard_map/tkd,df->tkf/dot_general | solution.py:24
  54.8 5.0 %convolution_bitcast_fusion.1 = f32[512,2,1,1792]{3,0,1,2:T(8,128)} fusion(bf16[512,2,512]{2,0,1:T(8,128)(2,1)S(1)} %constant_dynamic-update-slice_fusion, bf16[512,1792]{1,0:T(8,128)(2,1)S(1)} %copy-done.1), kind=kOutput, calls=%fused_computation.2 | convolution fusion | flops 1879048192 | bytes 10223616 | tf_op jit(solution)/shard_map/tkd,df->tkf/dot_general | solution.py:23
  59.8 11.9 %pad_maximum_fusion = f32[512,2,2,1792]{3,0,1,2:T(8,128)} fusion(f32[512,2,1,1792]{3,0,1,2:T(8,128)} %convolution_bitcast_fusion, f32[512,2,1,1792]{3,0,1,2:T(8,128)} %convolution_bitcast_fusion.1), kind=kLoop, calls=%fused_computation | loop fusion | flops 3670016 | bytes 29360128 | tf_op jit(solution)/shard_map/stack | solution.py:25
  71.8 0.0 all-gather.2.cloned.1.call-start
  71.8 0.8 dynamic-slice_compare_fusion
  72.6 106.7 %reduce-scatter.3.cloned.1.call-done = f32[32,2,2,1792]{3,0,1,2:T(8,128)} async-done(((f32[512,2,2,1792]{3,0,1,2:T(8,128)}), f32[32,2,2,1792]{3,0,1,2:T(8,128)}) %reduce-scatter.3.cloned.1.call-update) | async-done | bytes 917520 | tf_op jit(solution)/shard_map/reduce_scatter | solution.py:26
  179.3 1.3 fusion.5
  180.6 0.1 fusion.6
  180.7 0.7 pad_maximum_fusion.1
  181.4 0.0 reduce-scatter.5.cloned.1.call-start
  181.4 54.0 %all-gather.2.cloned.1.call-done = bf16[512,2,1792]{2,0,1:T(8,128)(2,1)} async-done(((bf16[32,2,1792]{2,0,1:T(8,128)(2,1)}), bf16[512,2,1792]{2,0,1:T(8,128)(2,1)}) %all-gather.2.cloned.1.call-update) | async-done | bytes 3670032 | tf_op jit(solution)/shard_map/all_gather | solution.py:32
  235.4 6.0 %fusion = f32[512,2,512]{2,0,1:T(8,128)} fusion(bf16[512,2,1792]{2,0,1:T(8,128)(2,1)} %all-gather.2.cloned.1.call-done, bf16[1792,512]{1,0:T(8,128)(2,1)} %param.11), kind=kOutput, calls=%fused_computation.3 | convolution fusion | flops 1879048192 | bytes 7602176 | tf_op jit(solution)/shard_map/tkf,fd->tkd/dot_general | solution.py:34
  241.4 59.8 %reduce-scatter.5.cloned.1.call-done = f32[32,2,512]{2,0,1:T(8,128)} async-done(((f32[512,2,512]{2,0,1:T(8,128)}), f32[32,2,512]{2,0,1:T(8,128)}) %reduce-scatter.5.cloned.1.call-update) | async-done | bytes 131088 | tf_op jit(solution)/shard_map/reduce_scatter | solution.py:33
  301.3 1.5 slice_bitcast_fusion.2
  (37 shorter events, 0.3 us)
Async XLA Ops:
  7.2 42.6 %copy-start = (bf16[512,1792]{1,0:T(8,128)(2,1)S(1)}, bf16[512,1792]{1,0:T(8,128)(2,1)}, u32[]{:S(2)}) copy-start(bf16[512,1792]{1,0:T(8,128)(2,1)} %param.10) | copy-start | bytes 5505028
  7.2 172.1 %reduce-scatter.3.cloned.1.call-start = ((), (), s32[]{:S(2)}) async-start(), calls=%async_computation.2 | async-start | bytes 15597568 | tf_op jit(solution)/shard_map/reduce_scatter | solution.py:26
  8.2 7.3 %collective-permute-start = (bf16[32,2,512]{2,0,1:T(8,128)(2,1)S(1)}, bf16[32,2,512]{2,0,1:T(8,128)(2,1)S(1)}, u32[]{:S(2)}, u32[]{:S(2)}) collective-permute-start(bf16[32,2,512]{2,0,1:T(8,128)(2,1)S(1)} %get-tuple-element.6), channel_id=1, source_target_pairs={{0,16},{16,32},{32,48},{48,64},{64,80},{80,96},{96,112},{112,128},... | collective-permute-start | bytes 196616 | tf_op jit(solution)/shard_map/ppermute | solution.py:16
  8.2 7.2 %collective-permute-start.1 = (bf16[32,2,512]{2,0,1:T(8,128)(2,1)S(1)}, bf16[32,2,512]{2,0,1:T(8,128)(2,1)S(1)}, u32[]{:S(2)}, u32[]{:S(2)}) collective-permute-start(bf16[32,2,512]{2,0,1:T(8,128)(2,1)S(1)} %get-tuple-element.6), channel_id=1, source_target_pairs={{0,240},{16,0},{32,16},{48,32},{64,48},{80,64},{96,80},{112,96},{1... | collective-permute-start | bytes 196616 | tf_op jit(solution)/shard_map/ppermute | solution.py:19
  15.5 4.9 %collective-permute-start.2 = (bf16[32,2,512]{2,0,1:T(8,128)(2,1)S(1)}, bf16[32,2,512]{2,0,1:T(8,128)(2,1)S(1)}, u32[]{:S(2)}, u32[]{:S(2)}) collective-permute-start(bf16[32,2,512]{2,0,1:T(8,128)(2,1)S(1)} %collective-permute-done), channel_id=1, source_target_pairs={{0,16},{16,32},{32,48},{48,64},{64,80},{80,96},{96,112},{112,128},... | collective-permute-start | bytes 196616 | tf_op jit(solution)/shard_map/ppermute | solution.py:16
  15.5 4.9 %collective-permute-start.3 = (bf16[32,2,512]{2,0,1:T(8,128)(2,1)S(1)}, bf16[32,2,512]{2,0,1:T(8,128)(2,1)S(1)}, u32[]{:S(2)}, u32[]{:S(2)}) collective-permute-start(bf16[32,2,512]{2,0,1:T(8,128)(2,1)S(1)} %collective-permute-done.1), channel_id=1, source_target_pairs={{0,240},{16,0},{32,16},{48,32},{64,48},{80,64},{96,80},{112,96},{1... | collective-permute-start | bytes 196616 | tf_op jit(solution)/shard_map/ppermute | solution.py:19
  20.4 4.9 %collective-permute-start.4 = (bf16[32,2,512]{2,0,1:T(8,128)(2,1)S(1)}, bf16[32,2,512]{2,0,1:T(8,128)(2,1)S(1)}, u32[]{:S(2)}, u32[]{:S(2)}) collective-permute-start(bf16[32,2,512]{2,0,1:T(8,128)(2,1)S(1)} %collective-permute-done.2), channel_id=1, source_target_pairs={{0,16},{16,32},{32,48},{48,64},{64,80},{80,96},{96,112},{112,128},... | collective-permute-start | bytes 196616 | tf_op jit(solution)/shard_map/ppermute | solution.py:16
  20.4 4.9 %collective-permute-start.5 = (bf16[32,2,512]{2,0,1:T(8,128)(2,1)S(1)}, bf16[32,2,512]{2,0,1:T(8,128)(2,1)S(1)}, u32[]{:S(2)}, u32[]{:S(2)}) collective-permute-start(bf16[32,2,512]{2,0,1:T(8,128)(2,1)S(1)} %collective-permute-done.3), channel_id=1, source_target_pairs={{0,240},{16,0},{32,16},{48,32},{64,48},{80,64},{96,80},{112,96},{1... | collective-permute-start | bytes 196616 | tf_op jit(solution)/shard_map/ppermute | solution.py:19
  25.3 4.9 %collective-permute-start.6 = (bf16[32,2,512]{2,0,1:T(8,128)(2,1)S(1)}, bf16[32,2,512]{2,0,1:T(8,128)(2,1)S(1)}, u32[]{:S(2)}, u32[]{:S(2)}) collective-permute-start(bf16[32,2,512]{2,0,1:T(8,128)(2,1)S(1)} %collective-permute-done.4), channel_id=1, source_target_pairs={{0,16},{16,32},{32,48},{48,64},{64,80},{80,96},{96,112},{112,128},... | collective-permute-start | bytes 196616 | tf_op jit(solution)/shard_map/ppermute | solution.py:16
  25.3 4.9 %collective-permute-start.7 = (bf16[32,2,512]{2,0,1:T(8,128)(2,1)S(1)}, bf16[32,2,512]{2,0,1:T(8,128)(2,1)S(1)}, u32[]{:S(2)}, u32[]{:S(2)}) collective-permute-start(bf16[32,2,512]{2,0,1:T(8,128)(2,1)S(1)} %collective-permute-done.5), channel_id=1, source_target_pairs={{0,240},{16,0},{32,16},{48,32},{64,48},{80,64},{96,80},{112,96},{1... | collective-permute-start | bytes 196616 | tf_op jit(solution)/shard_map/ppermute | solution.py:19
  30.2 4.9 %collective-permute-start.8 = (bf16[32,2,512]{2,0,1:T(8,128)(2,1)S(1)}, bf16[32,2,512]{2,0,1:T(8,128)(2,1)S(1)}, u32[]{:S(2)}, u32[]{:S(2)}) collective-permute-start(bf16[32,2,512]{2,0,1:T(8,128)(2,1)S(1)} %collective-permute-done.6), channel_id=1, source_target_pairs={{0,16},{16,32},{32,48},{48,64},{64,80},{80,96},{96,112},{112,128},... | collective-permute-start | bytes 196616 | tf_op jit(solution)/shard_map/ppermute | solution.py:16
  30.2 4.9 %collective-permute-start.9 = (bf16[32,2,512]{2,0,1:T(8,128)(2,1)S(1)}, bf16[32,2,512]{2,0,1:T(8,128)(2,1)S(1)}, u32[]{:S(2)}, u32[]{:S(2)}) collective-permute-start(bf16[32,2,512]{2,0,1:T(8,128)(2,1)S(1)} %collective-permute-done.7), channel_id=1, source_target_pairs={{0,240},{16,0},{32,16},{48,32},{64,48},{80,64},{96,80},{112,96},{1... | collective-permute-start | bytes 196616 | tf_op jit(solution)/shard_map/ppermute | solution.py:19
  35.1 4.9 %collective-permute-start.10 = (bf16[32,2,512]{2,0,1:T(8,128)(2,1)S(1)}, bf16[32,2,512]{2,0,1:T(8,128)(2,1)S(1)}, u32[]{:S(2)}, u32[]{:S(2)}) collective-permute-start(bf16[32,2,512]{2,0,1:T(8,128)(2,1)S(1)} %collective-permute-done.8), channel_id=1, source_target_pairs={{0,16},{16,32},{32,48},{48,64},{64,80},{80,96},{96,112},{112,128},... | collective-permute-start | bytes 196616 | tf_op jit(solution)/shard_map/ppermute | solution.py:16
  35.1 4.9 %collective-permute-start.11 = (bf16[32,2,512]{2,0,1:T(8,128)(2,1)S(1)}, bf16[32,2,512]{2,0,1:T(8,128)(2,1)S(1)}, u32[]{:S(2)}, u32[]{:S(2)}) collective-permute-start(bf16[32,2,512]{2,0,1:T(8,128)(2,1)S(1)} %collective-permute-done.9), channel_id=1, source_target_pairs={{0,240},{16,0},{32,16},{48,32},{64,48},{80,64},{96,80},{112,96},{1... | collective-permute-start | bytes 196616 | tf_op jit(solution)/shard_map/ppermute | solution.py:19
  40.0 4.9 %collective-permute-start.12 = (bf16[32,2,512]{2,0,1:T(8,128)(2,1)S(1)}, bf16[32,2,512]{2,0,1:T(8,128)(2,1)S(1)}, u32[]{:S(2)}, u32[]{:S(2)}) collective-permute-start(bf16[32,2,512]{2,0,1:T(8,128)(2,1)S(1)} %collective-permute-done.10), channel_id=1, source_target_pairs={{0,16},{16,32},{32,48},{48,64},{64,80},{80,96},{96,112},{112,128},... | collective-permute-start | bytes 196616 | tf_op jit(solution)/shard_map/ppermute | solution.py:16
  40.0 4.9 %collective-permute-start.13 = (bf16[32,2,512]{2,0,1:T(8,128)(2,1)S(1)}, bf16[32,2,512]{2,0,1:T(8,128)(2,1)S(1)}, u32[]{:S(2)}, u32[]{:S(2)}) collective-permute-start(bf16[32,2,512]{2,0,1:T(8,128)(2,1)S(1)} %collective-permute-done.11), channel_id=1, source_target_pairs={{0,240},{16,0},{32,16},{48,32},{64,48},{80,64},{96,80},{112,96},{1... | collective-permute-start | bytes 196616 | tf_op jit(solution)/shard_map/ppermute | solution.py:19
  44.9 4.9 %collective-permute-start.14 = (bf16[32,2,512]{2,0,1:T(8,128)(2,1)S(1)}, bf16[32,2,512]{2,0,1:T(8,128)(2,1)S(1)}, u32[]{:S(2)}, u32[]{:S(2)}) collective-permute-start(bf16[32,2,512]{2,0,1:T(8,128)(2,1)S(1)} %collective-permute-done.12), channel_id=1, source_target_pairs={{0,16},{16,32},{32,48},{48,64},{64,80},{80,96},{96,112},{112,128},... | collective-permute-start | bytes 196616 | tf_op jit(solution)/shard_map/ppermute | solution.py:16
  49.8 5.0 %copy-start.1 = (bf16[512,1792]{1,0:T(8,128)(2,1)S(1)}, bf16[512,1792]{1,0:T(8,128)(2,1)}, u32[]{:S(2)}) copy-start(bf16[512,1792]{1,0:T(8,128)(2,1)} %param.9) | copy-start | bytes 5505028
  71.8 163.6 %all-gather.2.cloned.1.call-start = ((), (), s32[]{:S(2)}) async-start(), calls=%async_computation.3 | async-start | bytes 3899392 | tf_op jit(solution)/shard_map/all_gather | solution.py:32
  181.4 119.9 %reduce-scatter.5.cloned.1.call-start = ((), (), s32[]{:S(2)}) async-start(), calls=%async_computation.4 | async-start | bytes 2228224 | tf_op jit(solution)/shard_map/reduce_scatter | solution.py:33
Sparse Core Ops, SparseCore 0:
  71.9 107.3 reduce-scatter.2
  181.7 53.6 all-gather.1
  241.6 59.6 reduce-scatter.4
